TPU v7x, 512 devices: a whole 4x4x16 slice. The times are simulated.
512 devices in a mesh: segment: 64 (over y, x, z_hi, core), fsdp: 8 (over z_lo).
Axes of the slice: x: 4, y: 4, z: 16 (z_hi: 2, z_lo: 8; z = z_hi * 8 + z_lo), core: 2. Of those that a mesh axis runs over, the one named last changes fastest.
Arguments:
- stream: bfloat16 [2, 64, 512, 4096], P(None, 'segment', 'fsdp'), may hold values from -60 to 60
- gain: bfloat16 [2, 64, 4096], P(None, 'segment'), may hold values from 0.099609375 to 1.8984375
- w_query: bfloat16 [2, 64, 32, 128, 128], P(None, 'segment', 'fsdp'), may hold values from -20 to 20
- w_key: bfloat16 [2, 64, 32, 128, 128], P(None, 'segment', 'fsdp'), may hold values from -20 to 20
- w_value: bfloat16 [2, 64, 32, 128, 128], P(None, 'segment', 'fsdp'), may hold values from -0.5 to 0.5
- w_mix: bfloat16 [2, 64, 128, 32, 32], P(None, 'segment', 'fsdp'), may hold values from -1 to 1
- active: int32 [2, 64], P(None, 'segment'), may hold values from 0 to 1
- random_blocks: int32 [2, 64, 8, 2], P(None, 'segment'), may hold values from 0 to 7
Outputs:
- advanced: bfloat16 [2, 64, 512, 4096], P(None, 'segment', 'fsdp')
All inputs are finite; a program needn't handle non-finite values.
Results may differ from a plain program's by a relative error of at most 0.009.
Values may be sent and summed in bfloat16 or wider, within the bound.
No kernel may reach another device: no remote copies, remote signals or barrier semaphores. Data moves between devices by JAX's collectives and lax.ppermute only.
A program may use at most 64 MiB of HBM per device.

v0:
```python
import jax
import jax.numpy as jnp
from jax import lax
from jax.sharding import PartitionSpec as P

BLK = 64
ROUNDS = 2
EPS = 1e-05


def shifted(value, axis, by):
    devices = lax.axis_size(axis)
    return lax.ppermute(value, axis, [(i, (i + by) % devices) for i in range(devices)])


def block_attention(query, keys, values, random_ids):
    heads, seq_len, head_width = query.shape
    count = seq_len // BLK
    query_blocks = query.reshape(heads, count, BLK, head_width)
    key_blocks = keys.reshape(heads, count, BLK, head_width)
    value_blocks = values.reshape(heads, count, BLK, head_width)
    block_ids = jnp.arange(count, dtype=jnp.int32)
    window = jnp.stack(
        [(block_ids - 1) % count, block_ids, (block_ids + 1) % count, jnp.zeros_like(block_ids)],
        axis=1,
    )
    chosen = jnp.concatenate([window, random_ids], axis=1)
    picked_keys = key_blocks[:, chosen].reshape(heads, count, chosen.shape[1] * BLK, head_width)
    picked_values = value_blocks[:, chosen].reshape(heads, count, chosen.shape[1] * BLK, head_width)
    scores = jnp.einsum(
        "hnqd,hnkd->hnqk", query_blocks, picked_keys, preferred_element_type=jnp.float32
    )
    row_max = jnp.max(scores, axis=-1, keepdims=True)
    powers = jnp.exp(scores - row_max)
    weights = (powers / jnp.sum(powers, axis=-1, keepdims=True)).astype(jnp.bfloat16)
    mixed = jnp.einsum(
        "hnqk,hnkd->hnqd", weights, picked_values, preferred_element_type=jnp.float32
    ).astype(jnp.bfloat16)
    return mixed.reshape(heads, seq_len, head_width)


def head_attention(view, queries_w, keys_w, values_w, random_ids):

    def one_segment(items):
        rows, weight_q, weight_k, weight_v, ids = items
        raw = jnp.einsum("thc,hcd->htd", rows, weight_q, preferred_element_type=jnp.float32)
        query = (raw * rows.shape[-1] ** (-0.5)).astype(jnp.bfloat16)
        keys = jnp.einsum(
            "thc,hcd->htd", rows, weight_k, preferred_element_type=jnp.float32
        ).astype(jnp.bfloat16)
        values = jnp.einsum(
            "thc,hcd->htd", rows, weight_v, preferred_element_type=jnp.float32
        ).astype(jnp.bfloat16)
        return block_attention(query, keys, values, ids)

    return lax.map(one_segment, (view, queries_w, keys_w, values_w, random_ids))


def mix_heads(attended, mix_w):
    return jnp.einsum(
        "vhtc,vchg->vtgc",
        attended,
        lax.all_gather(mix_w, "fsdp", axis=1, tiled=True),
        preferred_element_type=jnp.float32,
    ).astype(jnp.bfloat16)


def cycle(values):
    moved = shifted(values, "segment", 1)
    return jnp.where(lax.axis_index("segment") == 0, jnp.roll(moved, 1, axis=0), moved)


def token_layer(state, params):
    queries_w, keys_w, values_w, mix_w, gains, live, random_ids = params
    wide = state.astype(jnp.float32)
    mean_sq = jnp.mean(wide * wide, axis=2, keepdims=True)
    normed = (wide * lax.rsqrt(mean_sq + EPS) * gains[:, None, :].astype(jnp.float32)).astype(
        jnp.bfloat16
    )
    view = normed.reshape(state.shape[0], state.shape[1], -1, queries_w.shape[-1])
    gathered = lax.all_to_all(view, "fsdp", split_axis=2, concat_axis=1, tiled=True)
    attended = head_attention(gathered, queries_w, keys_w, values_w, random_ids)
    returned = lax.all_to_all(attended, "fsdp", split_axis=2, concat_axis=1, tiled=True)
    mixed = mix_heads(returned, mix_w)
    updated = (wide + mixed.reshape(wide.shape).astype(jnp.float32)).astype(jnp.bfloat16)
    return jnp.where(live[:, None, None] > 0, updated, state)


def shards(stream, gain, w_query, w_key, w_value, w_mix, active, random_blocks):
    params = (
        w_query[:, 0],
        w_key[:, 0],
        w_value[:, 0],
        w_mix[:, 0],
        gain[:, 0],
        active[:, 0],
        random_blocks[:, 0],
    )
    state = stream[:, 0]
    for round_index in range(ROUNDS):
        state = token_layer(state, params)
        state = cycle(state)
    return state[:, None]


def solution(mesh):
    in_specs = (
        P(None, "segment", "fsdp", None),
        P(None, "segment", None),
        P(None, "segment", "fsdp", None, None),
        P(None, "segment", "fsdp", None, None),
        P(None, "segment", "fsdp", None, None),
        P(None, "segment", "fsdp", None, None),
        P(None, "segment"),
        P(None, "segment", None, None),
    )
    out_specs = P(None, "segment", "fsdp", None)
    return jax.shard_map(shards, mesh=mesh, in_specs=in_specs, out_specs=out_specs, check_vma=False)
```

profile of v0, /device:TPU:32, one launch (start us, length us, event | category | flops | bytes accessed | tf_op | source)
XLA Modules:
  0.0 546.5 jit_solution(105183954423557872)
XLA Ops:
  5.5 12.8 %all-to-all-start = ((bf16[2,64,32,128]{3,1,0,2:T(8,128)(2,1)}), bf16[2,64,32,128]{3,1,0,2:T(8,128)(2,1)S(1)}, u32[]{:S(2)}, u32[]{:S(2)}) async-start(bf16[2,64,32,128]{3,1,0,2:T(8,128)(2,1)} %copy.69), calls=%async_computation | async-start | bytes 2097152 | tf_op jit(solution)/shard_map/all_to_all | solution.py:81
  18.3 48.3 %all-to-all-done = bf16[2,64,32,128]{3,1,0,2:T(8,128)(2,1)S(1)} async-done(((bf16[2,64,32,128]{3,1,0,2:T(8,128)(2,1)}), bf16[2,64,32,128]{3,1,0,2:T(8,128)(2,1)S(1)}, u32[]{:S(2)}, u32[]{:S(2)}) %all-to-all-start) | async-done | bytes 1048608 | tf_op jit(solution)/shard_map/all_to_all | solution.py:81
  68.9 56.5 %while.24 = (s32[]{:T(128)}, bf16[2,4,512,128]{3,1,0,2:T(4,128)(2,1)}, bf16[2,512,4,128]{3,1,2,0:T(8,128)(2,1)}, bf16[2,4,128,128]{3,2,1,0:T(8,128)(2,1)S(1)}, b...) while((s32[]{:T(128)}, ...), condition=%wide.region_4.5_spmd, body=%wide.region_1.4_spmd.sunk | while | flops 609226816 | bytes 59140032 | solution.py:56
  73.3 2.9 copy.106
  82.0 2.7 gather_fusion
  84.8 2.9 copy.105
  87.6 7.3 %fusion.139 = bf16[4,8,64,128]{3,2,1,0:T(8,128)(2,1)} fusion(bf16[4,8,384,128]{3,2,1,0:T(8,128)(2,1)S(1)} %bitcast.258, f32[4,8,64]{2,1,0:T(8,128)S(1)} %fusion.138, f32[4,8,64,384]{3,2,1,0:T(8,128)} %copy-done), kind=kOutput, calls=%fused_computation.9.clone.1 | convolution fusion | flops 203950464 | bytes 6823936 | tf_op jit(solution)/shard_map/while/body/eval_jaxpr/hnqk,hnkd->hnqd/dot_general | solution.py:36
  101.5 2.9 copy.106
  110.3 2.7 gather_fusion
  113.0 2.9 copy.105
  115.9 7.3 %fusion.139 = bf16[4,8,64,128]{3,2,1,0:T(8,128)(2,1)} fusion(bf16[4,8,384,128]{3,2,1,0:T(8,128)(2,1)S(1)} %bitcast.258, f32[4,8,64]{2,1,0:T(8,128)S(1)} %fusion.138, f32[4,8,64,384]{3,2,1,0:T(8,128)} %copy-done), kind=kOutput, calls=%fused_computation.9.clone.1 | convolution fusion | flops 203950464 | bytes 6823936 | tf_op jit(solution)/shard_map/while/body/eval_jaxpr/hnqk,hnkd->hnqd/dot_general | solution.py:36
  125.4 7.2 %all-to-all-start.1 = ((bf16[2,4,512,128]{3,1,0,2:T(4,128)(2,1)}), bf16[2,4,512,128]{3,1,0,2:T(4,128)(2,1)S(1)}, u32[]{:S(2)}, u32[]{:S(2)}) async-start(bf16[2,4,512,128]{3,1,0,2:T(4,128)(2,1)} %get-tuple-element.187), calls=%async_computation.1 | async-start | bytes 2097152 | tf_op jit(solution)/shard_map/all_to_all | solution.py:83
  134.4 89.3 %all-gather = bf16[2,1,128,32,32]{3,4,2,0,1:T(8,128)(2,1)S(1)} all-gather(bf16[2,1,16,32,32]{3,4,2,0,1:T(8,128)(2,1)} %copy.74), channel_id=2, replica_groups=mesh['segment'=64,'fsdp'=8] {'fsdp'}, dimensions={2}, use_global_device_ids=true | all-gather | bytes 589824 | tf_op jit(solution)/shard_map/all_gather | solution.py:63
  223.7 3.3 copy.73
  227.0 4.2 convert_bitcast_fusion.1
  231.2 5.3 copy.75
  241.7 51.0 %collective-permute-done = bf16[2,64,4096]{2,1,0:T(8,128)(2,1)S(1)} collective-permute-done((bf16[2,64,4096]{2,1,0:T(8,128)(2,1)}, bf16[2,64,4096]{2,1,0:T(8,128)(2,1)S(1)}, u32[]{:S(2)}, u32[]{:S(2)}) %collective-permute-start) | collective-permute-done | bytes 1048608 | tf_op jit(solution)/shard_map/ppermute | solution.py:13
  295.6 19.6 %all-to-all-start.2 = ((bf16[2,64,32,128]{3,1,0,2:T(8,128)(2,1)}), bf16[2,64,32,128]{3,1,0,2:T(8,128)(2,1)S(1)}, u32[]{:S(2)}, u32[]{:S(2)}) async-start(bf16[2,64,32,128]{3,1,0,2:T(8,128)(2,1)} %copy_bitcast_fusion), calls=%async_computation.2 | async-start | bytes 2097152 | tf_op jit(solution)/shard_map/all_to_all | solution.py:81
  315.2 38.3 %all-to-all-done.2 = bf16[2,64,32,128]{3,1,0,2:T(8,128)(2,1)S(1)} async-done(((bf16[2,64,32,128]{3,1,0,2:T(8,128)(2,1)}), bf16[2,64,32,128]{3,1,0,2:T(8,128)(2,1)S(1)}, u32[]{:S(2)}, u32[]{:S(2)}) %all-to-all-start.2) | async-done | bytes 1048608 | tf_op jit(solution)/shard_map/all_to_all | solution.py:81
  355.8 56.6 %while.25 = (s32[]{:T(128)}, bf16[2,4,512,128]{3,1,0,2:T(4,128)(2,1)}, bf16[2,512,4,128]{3,1,2,0:T(8,128)(2,1)}, bf16[2,4,128,128]{3,2,1,0:T(8,128)(2,1)S(1)}, b...) while((s32[]{:T(128)}, ...), condition=%wide.region_9.10_spmd, body=%wide.region_6.9_spmd.sunk | while | flops 609226816 | bytes 59140032 | solution.py:56
  360.1 2.9 copy.110
  371.6 2.9 copy.109
  374.5 7.3 %fusion.156 = bf16[4,8,64,128]{3,2,1,0:T(8,128)(2,1)} fusion(bf16[4,8,384,128]{3,2,1,0:T(8,128)(2,1)S(1)} %bitcast.259, f32[4,8,64]{2,1,0:T(8,128)S(1)} %fusion.155, f32[4,8,64,384]{3,2,1,0:T(8,128)} %copy-done.1), kind=kOutput, calls=%fused_computation.49.clone.1 | convolution fusion | flops 203950464 | bytes 6823936 | tf_op jit(solution)/shard_map/while/body/eval_jaxpr/hnqk,hnkd->hnqd/dot_general | solution.py:36
  388.4 2.9 copy.110
  397.2 2.7 gather_fusion.2
  399.9 2.9 copy.109
  402.8 7.3 %fusion.156 = bf16[4,8,64,128]{3,2,1,0:T(8,128)(2,1)} fusion(bf16[4,8,384,128]{3,2,1,0:T(8,128)(2,1)S(1)} %bitcast.259, f32[4,8,64]{2,1,0:T(8,128)S(1)} %fusion.155, f32[4,8,64,384]{3,2,1,0:T(8,128)} %copy-done.1), kind=kOutput, calls=%fused_computation.49.clone.1 | convolution fusion | flops 203950464 | bytes 6823936 | tf_op jit(solution)/shard_map/while/body/eval_jaxpr/hnqk,hnkd->hnqd/dot_general | solution.py:36
  412.4 55.1 %all_to_all.72 = bf16[2,4,512,128]{3,1,0,2:T(4,128)(2,1)S(1)} all-to-all(bf16[2,4,512,128]{3,1,0,2:T(4,128)(2,1)} %get-tuple-element.188), channel_id=1, replica_groups=mesh['segment'=64,'fsdp'=8] {'fsdp'}, dimensions={2} | all-to-all | bytes 2097152 | tf_op jit(solution)/shard_map/all_to_all | solution.py:83
  467.5 3.2 copy.79
  470.7 4.2 convert_bitcast_fusion
  474.9 4.5 copy.80
  484.9 60.4 %collective-permute-done.1 = bf16[2,64,4096]{2,1,0:T(8,128)(2,1)S(1)} collective-permute-done((bf16[2,64,4096]{2,1,0:T(8,128)(2,1)S(1)}, bf16[2,64,4096]{2,1,0:T(8,128)(2,1)S(1)}, u32[]{:S(2)}, u32[]{:S(2)}) %collective-permute-start.1) | collective-permute-done | bytes 1048608 | tf_op jit(solution)/shard_map/ppermute | solution.py:13
  (115 shorter events, 78.9 us)
Async XLA Ops:
  5.5 63.4 %copy-start.7 = (bf16[2,1,4,128,128]{4,3,2,1,0:T(8,128)(2,1)S(1)}, bf16[2,1,4,128,128]{4,3,2,1,0:T(8,128)(2,1)}, u32[]{:S(2)}) copy-start(bf16[2,1,4,128,128]{4,3,2,1,0:T(8,128)(2,1)} %param.14) | copy-start | bytes 786436
  5.5 63.4 %copy-start.8 = (s32[2,1,8,2]{2,3,1,0:T(2,128)S(1)}, s32[2,1,8,2]{2,3,1,0:T(2,128)}, u32[]{:S(2)}) copy-start(s32[2,1,8,2]{2,3,1,0:T(2,128)} %param.19) | copy-start | bytes 388
  5.5 61.1 %all-to-all-start = ((bf16[2,64,32,128]{3,1,0,2:T(8,128)(2,1)}), bf16[2,64,32,128]{3,1,0,2:T(8,128)(2,1)S(1)}, u32[]{:S(2)}, u32[]{:S(2)}) async-start(bf16[2,64,32,128]{3,1,0,2:T(8,128)(2,1)} %copy.69), calls=%async_computation | async-start | bytes 2097152 | tf_op jit(solution)/shard_map/all_to_all | solution.py:81
  68.9 65.4 %copy-start.9 = (s32[2,1]{0,1:T(1,128)S(1)}, s32[2,1]{0,1:T(1,128)}, u32[]{:S(2)}) copy-start(s32[2,1]{0,1:T(1,128)} %param.18) | copy-start | bytes 28
  79.0 1.7 copy-start
  107.3 1.7 copy-start
  125.4 98.2 %all-to-all-start.1 = ((bf16[2,4,512,128]{3,1,0,2:T(4,128)(2,1)}), bf16[2,4,512,128]{3,1,0,2:T(4,128)(2,1)S(1)}, u32[]{:S(2)}, u32[]{:S(2)}) async-start(bf16[2,4,512,128]{3,1,0,2:T(4,128)(2,1)} %get-tuple-element.187), calls=%async_computation.1 | async-start | bytes 2097152 | tf_op jit(solution)/shard_map/all_to_all | solution.py:83
  223.7 7.6 %copy-start.2 = (bf16[2,1,128,32,32]{3,4,2,0,1:T(8,128)(2,1)}, bf16[2,1,128,32,32]{3,4,2,0,1:T(8,128)(2,1)S(1)}, u32[]{:S(2)}) copy-start(bf16[2,1,128,32,32]{3,4,2,0,1:T(8,128)(2,1)S(1)} %all-gather) | copy-start | bytes 1572868
  236.5 1.9 copy-start.4
  239.8 52.9 %collective-permute-start = (bf16[2,64,4096]{2,1,0:T(8,128)(2,1)}, bf16[2,64,4096]{2,1,0:T(8,128)(2,1)S(1)}, u32[]{:S(2)}, u32[]{:S(2)}) collective-permute-start(bf16[2,64,4096]{2,1,0:T(8,128)(2,1)} %fusion.67), channel_id=1, source_target_pairs={{0,8},{8,16},{16,24},{24,32},{32,40},{40,48},{48,56},{56,64},{64,7... | collective-permute-start | bytes 3145736 | tf_op jit(solution)/shard_map/ppermute | solution.py:13
  293.2 1.0 copy-start.5
  295.6 57.8 %all-to-all-start.2 = ((bf16[2,64,32,128]{3,1,0,2:T(8,128)(2,1)}), bf16[2,64,32,128]{3,1,0,2:T(8,128)(2,1)S(1)}, u32[]{:S(2)}, u32[]{:S(2)}) async-start(bf16[2,64,32,128]{3,1,0,2:T(8,128)(2,1)} %copy_bitcast_fusion), calls=%async_computation.2 | async-start | bytes 2097152 | tf_op jit(solution)/shard_map/all_to_all | solution.py:81
  365.9 1.7 copy-start.1
  394.2 1.7 copy-start.1
  412.4 58.3 %copy-start.3 = (bf16[2,1,128,32,32]{3,4,2,0,1:T(8,128)(2,1)S(1)}, bf16[2,1,128,32,32]{3,4,2,0,1:T(8,128)(2,1)}, u32[]{:S(2)}) copy-start(bf16[2,1,128,32,32]{3,4,2,0,1:T(8,128)(2,1)} %copy-done.2) | copy-start | bytes 1572868
  479.4 1.6 copy-start.6
  483.0 62.3 %collective-permute-start.1 = (bf16[2,64,4096]{2,1,0:T(8,128)(2,1)S(1)}, bf16[2,64,4096]{2,1,0:T(8,128)(2,1)S(1)}, u32[]{:S(2)}, u32[]{:S(2)}) collective-permute-start(bf16[2,64,4096]{2,1,0:T(8,128)(2,1)S(1)} %fusion.66), channel_id=1, source_target_pairs={{0,8},{8,16},{16,24},{24,32},{32,40},{40,48},{48,56},{56,64},{64,7... | collective-permute-start | bytes 3145736 | tf_op jit(solution)/shard_map/ppermute | solution.py:13
where the time goes:
time: 548 us; the launch traced here: 547 us
  waiting for transfers between devices  198 us (36%)
  blocking collectives  144 us (26%)
  local copies, waits for them, and re-layouts  85.7 us (16%)
  matrix products  59.8 us (11%)
  starting transfers between devices  43.3 us (8%)
  other arithmetic  14.7 us (3%)
    ppermute x2, waiting for transfers between devices, shifted(): lax.ppermute(value, axis, [(i, (i + by) % devices) for i in range(devices)])  111 us
    all_gather x1, blocking collectives, mix_heads(): lax.all_gather(mix_w, 'fsdp', axis=1, tiled=True)  89.3 us
    all_to_all x2, waiting for transfers between devices, token_layer(): lax.all_to_all(view, 'fsdp', split_axis=2, concat_axis=1, tiled=True)  86.6 us
    all_to_all x1, blocking collectives, token_layer(): lax.all_to_all(attended, 'fsdp', split_axis=2, concat_axis=1, tiled=True)  55.1 us
    all_to_all x2, starting transfers between devices, token_layer(): lax.all_to_all(view, 'fsdp', split_axis=2, concat_axis=1, tiled=True)  32.4 us
    dot_general x4, matrix products, block_attention(): jnp.einsum('hnqk,hnkd->hnqd', weights, picked_values, preferred_element_t...  29.3 us
    gather x8, local copies, waits for them, and re-layouts, block_attention(): value_blocks[:, chosen]  22.4 us
    gather x8, local copies, waits for them, and re-layouts, block_attention(): key_blocks[:, chosen]  22.3 us
  transfers between devices with their start and end apart: 5, of which 4 were waited for; matrix products, arithmetic and copies ran while one was open for 0% of the time, Pallas kernels for 0%

commit v1 on v0

--- a/solution.py
+++ b/solution.py
@@ -6,6 +6,18 @@
 BLK = 64
 ROUNDS = 2
 EPS = 1e-05
+
+
+def slot_list(load, axis_name, along_dim, on_dim):
+    return jnp.concatenate(
+        jax.lax.all_to_all(
+            jnp.stack(jnp.split(load, jax.lax.axis_size(axis_name), axis=along_dim), axis=0),
+            axis_name,
+            0,
+            0,
+        ),
+        axis=on_dim,
+    )
 
 
 def shifted(value, axis, by):
@@ -80,7 +92,7 @@
     view = normed.reshape(state.shape[0], state.shape[1], -1, queries_w.shape[-1])
     gathered = lax.all_to_all(view, "fsdp", split_axis=2, concat_axis=1, tiled=True)
     attended = head_attention(gathered, queries_w, keys_w, values_w, random_ids)
-    returned = lax.all_to_all(attended, "fsdp", split_axis=2, concat_axis=1, tiled=True)
+    returned = slot_list(attended, "fsdp", 2, 1)
     mixed = mix_heads(returned, mix_w)
     updated = (wide + mixed.reshape(wide.shape).astype(jnp.float32)).astype(jnp.bfloat16)
     return jnp.where(live[:, None, None] > 0, updated, state)

time: 548 us -> 566 us (1.033)
  local copies, waits for them, and re-layouts: 85.7 us -> 103 us
    unnamed x19 -> x35, local copies, waits for them, and re-layouts: 4.28 us -> 20.9 us
    all_to_all x2 -> x0, local copies, waits for them, and re-layouts: 6.55 us -> none  [token_layer(): lax.all_to_all(attended, 'fsdp', split_axis=2, concat_axis=1, tiled=True)]
    reshape x0 -> x2, local copies, waits for them, and re-layouts: none -> 6.19 us  [slot_list(): jnp.concatenate(jax.lax.all_to_all(jnp.stack(jnp.split(load, jax.lax.axis...]
where the time goes in v1:
time: 566 us; the launch traced here: 564 us
  waiting for transfers between devices  198 us (35%)
  blocking collectives  145 us (26%)
  local copies, waits for them, and re-layouts  103 us (18%)
  matrix products  59.8 us (11%)
  starting transfers between devices  43.3 us (8%)
  other arithmetic  14.7 us (3%)
    ppermute x2, waiting for transfers between devices, shifted(): lax.ppermute(value, axis, [(i, (i + by) % devices) for i in range(devices)])  111 us
    all_gather x1, blocking collectives, mix_heads(): lax.all_gather(mix_w, 'fsdp', axis=1, tiled=True)  90.2 us
    all_to_all x2, waiting for transfers between devices, token_layer(): lax.all_to_all(view, 'fsdp', split_axis=2, concat_axis=1, tiled=True)  86.6 us
    all_to_all x1, blocking collectives, slot_list(): jax.lax.all_to_all(jnp.stack(jnp.split(load, jax.lax.axis_size(axis_name)...  54.8 us
    all_to_all x2, starting transfers between devices, token_layer(): lax.all_to_all(view, 'fsdp', split_axis=2, concat_axis=1, tiled=True)  32.4 us
    dot_general x4, matrix products, block_attention(): jnp.einsum('hnqk,hnkd->hnqd', weights, picked_values, preferred_element_t...  29.2 us
    gather x8, local copies, waits for them, and re-layouts, block_attention(): value_blocks[:, chosen]  22.4 us
    gather x8, local copies, waits for them, and re-layouts, block_attention(): key_blocks[:, chosen]  22.3 us
  transfers between devices with their start and end apart: 5, of which 4 were waited for; matrix products, arithmetic and copies ran while one was open for 0% of the time, Pallas kernels for 0%

profile of v1, /device:TPU:32, one launch (start us, length us, event | category | flops | bytes accessed | tf_op | source)
XLA Modules:
  0.0 563.9 jit_solution(13023628430575466286)
XLA Ops:
  5.5 12.8 %all-to-all-start = ((bf16[2,64,32,128]{3,1,0,2:T(8,128)(2,1)}), bf16[2,64,32,128]{3,1,0,2:T(8,128)(2,1)S(1)}, u32[]{:S(2)}, u32[]{:S(2)}) async-start(bf16[2,64,32,128]{3,1,0,2:T(8,128)(2,1)} %copy.69), calls=%async_computation | async-start | bytes 2097152 | tf_op jit(solution)/shard_map/all_to_all | solution.py:93
  18.3 48.3 %all-to-all-done = bf16[2,64,32,128]{3,1,0,2:T(8,128)(2,1)S(1)} async-done(((bf16[2,64,32,128]{3,1,0,2:T(8,128)(2,1)}), bf16[2,64,32,128]{3,1,0,2:T(8,128)(2,1)S(1)}, u32[]{:S(2)}, u32[]{:S(2)}) %all-to-all-start) | async-done | bytes 1048608 | tf_op jit(solution)/shard_map/all_to_all | solution.py:93
  68.8 55.7 %while.24 = (s32[]{:T(128)}, bf16[2,4,512,128]{3,2,1,0:T(8,128)(2,1)}, bf16[2,512,4,128]{3,1,2,0:T(8,128)(2,1)}, bf16[2,4,128,128]{3,2,1,0:T(8,128)(2,1)S(1)}, b...) while((s32[]{:T(128)}, ...), condition=%wide.region_4.5_spmd, body=%wide.region_1.4_spmd.sunk | while | flops 609226816 | bytes 59140032 | solution.py:68
  73.1 2.9 copy.95
  81.9 2.7 gather_fusion
  84.6 2.9 copy.94
  87.5 7.3 %fusion.139 = bf16[4,8,64,128]{3,2,1,0:T(8,128)(2,1)} fusion(bf16[4,8,384,128]{3,2,1,0:T(8,128)(2,1)S(1)} %bitcast.286, f32[4,8,64]{2,1,0:T(8,128)S(1)} %fusion.138, f32[4,8,64,384]{3,2,1,0:T(8,128)} %copy-done), kind=kOutput, calls=%fused_computation.9.clone.1 | convolution fusion | flops 203950464 | bytes 6823936 | tf_op jit(solution)/shard_map/while/body/eval_jaxpr/hnqk,hnkd->hnqd/dot_general | solution.py:48
  101.0 2.9 copy.95
  112.4 2.9 copy.94
  115.3 7.3 %fusion.139 = bf16[4,8,64,128]{3,2,1,0:T(8,128)(2,1)} fusion(bf16[4,8,384,128]{3,2,1,0:T(8,128)(2,1)S(1)} %bitcast.286, f32[4,8,64]{2,1,0:T(8,128)S(1)} %fusion.138, f32[4,8,64,384]{3,2,1,0:T(8,128)} %copy-done), kind=kOutput, calls=%fused_computation.9.clone.1 | convolution fusion | flops 203950464 | bytes 6823936 | tf_op jit(solution)/shard_map/while/body/eval_jaxpr/hnqk,hnkd->hnqd/dot_general | solution.py:48
  137.0 7.2 %all-to-all-start.1 = ((bf16[8,2,4,64,128]{4,3,2,1,0:T(8,128)(2,1)}), bf16[8,2,4,64,128]{4,3,2,1,0:T(8,128)(2,1)S(1)}, u32[]{:S(2)}, u32[]{:S(2)}) async-start(bf16[8,2,4,64,128]{4,3,2,1,0:T(8,128)(2,1)} %bitcast_dynamic-update-slice_fusion.8), calls=%async_computation.1 | async-start | bytes 2097152 | tf_op jit(solution)/shard_map/all_to_all | solution.py:13
  145.0 90.2 %all-gather = bf16[2,1,128,32,32]{3,4,2,0,1:T(8,128)(2,1)S(1)} all-gather(bf16[2,1,16,32,32]{3,4,2,0,1:T(8,128)(2,1)} %copy.73), channel_id=2, replica_groups=mesh['segment'=64,'fsdp'=8] {'fsdp'}, dimensions={2}, use_global_device_ids=true | all-gather | bytes 589824 | tf_op jit(solution)/shard_map/all_gather | solution.py:75
  235.2 3.2 copy.72
  238.5 4.2 convert_bitcast_fusion.1
  242.7 5.3 copy.74
  253.1 51.0 %collective-permute-done = bf16[2,64,4096]{2,1,0:T(8,128)(2,1)S(1)} collective-permute-done((bf16[2,64,4096]{2,1,0:T(8,128)(2,1)}, bf16[2,64,4096]{2,1,0:T(8,128)(2,1)S(1)}, u32[]{:S(2)}, u32[]{:S(2)}) %collective-permute-start) | collective-permute-done | bytes 1048608 | tf_op jit(solution)/shard_map/ppermute | solution.py:25
  307.0 19.6 %all-to-all-start.2 = ((bf16[2,64,32,128]{3,1,0,2:T(8,128)(2,1)}), bf16[2,64,32,128]{3,1,0,2:T(8,128)(2,1)S(1)}, u32[]{:S(2)}, u32[]{:S(2)}) async-start(bf16[2,64,32,128]{3,1,0,2:T(8,128)(2,1)} %copy_bitcast_fusion), calls=%async_computation.2 | async-start | bytes 2097152 | tf_op jit(solution)/shard_map/all_to_all | solution.py:93
  326.6 38.2 %all-to-all-done.2 = bf16[2,64,32,128]{3,1,0,2:T(8,128)(2,1)S(1)} async-done(((bf16[2,64,32,128]{3,1,0,2:T(8,128)(2,1)}), bf16[2,64,32,128]{3,1,0,2:T(8,128)(2,1)S(1)}, u32[]{:S(2)}, u32[]{:S(2)}) %all-to-all-start.2) | async-done | bytes 1048608 | tf_op jit(solution)/shard_map/all_to_all | solution.py:93
  367.1 55.6 %while.25 = (s32[]{:T(128)}, bf16[2,4,512,128]{3,2,1,0:T(8,128)(2,1)}, bf16[2,512,4,128]{3,1,2,0:T(8,128)(2,1)}, bf16[2,4,128,128]{3,2,1,0:T(8,128)(2,1)S(1)}, b...) while((s32[]{:T(128)}, ...), condition=%wide.region_9.10_spmd, body=%wide.region_6.9_spmd.sunk | while | flops 609226816 | bytes 59140032 | solution.py:68
  371.4 2.9 copy.98
  380.2 2.7 gather_fusion.2
  382.9 2.9 copy.97
  385.8 7.3 %fusion.156 = bf16[4,8,64,128]{3,2,1,0:T(8,128)(2,1)} fusion(bf16[4,8,384,128]{3,2,1,0:T(8,128)(2,1)S(1)} %bitcast.287, f32[4,8,64]{2,1,0:T(8,128)S(1)} %fusion.155, f32[4,8,64,384]{3,2,1,0:T(8,128)} %copy-done.1), kind=kOutput, calls=%fused_computation.49.clone.1 | convolution fusion | flops 203950464 | bytes 6823936 | tf_op jit(solution)/shard_map/while/body/eval_jaxpr/hnqk,hnkd->hnqd/dot_general | solution.py:48
  399.2 2.9 copy.98
  408.0 2.7 gather_fusion.2
  410.7 2.9 copy.97
  413.6 7.3 %fusion.156 = bf16[4,8,64,128]{3,2,1,0:T(8,128)(2,1)} fusion(bf16[4,8,384,128]{3,2,1,0:T(8,128)(2,1)S(1)} %bitcast.287, f32[4,8,64]{2,1,0:T(8,128)S(1)} %fusion.155, f32[4,8,64,384]{3,2,1,0:T(8,128)} %copy-done.1), kind=kOutput, calls=%fused_computation.49.clone.1 | convolution fusion | flops 203950464 | bytes 6823936 | tf_op jit(solution)/shard_map/while/body/eval_jaxpr/hnqk,hnkd->hnqd/dot_general | solution.py:48
  430.4 54.8 %all_to_all.46 = bf16[8,2,4,64,128]{4,3,2,1,0:T(8,128)(2,1)S(1)} all-to-all(bf16[8,2,4,64,128]{4,3,2,1,0:T(8,128)(2,1)S(1)} %bitcast_dynamic-update-slice_fusion), channel_id=1, replica_groups=mesh['segment'=64,'fsdp'=8] {'fsdp'}, dimensions={0} | all-to-all | bytes 2097152 | tf_op jit(solution)/shard_map/all_to_all | solution.py:13
  485.1 3.0 copy.77
  488.1 4.2 convert_bitcast_fusion
  492.3 4.5 copy.78
  502.3 60.4 %collective-permute-done.1 = bf16[2,64,4096]{2,1,0:T(8,128)(2,1)S(1)} collective-permute-done((bf16[2,64,4096]{2,1,0:T(8,128)(2,1)S(1)}, bf16[2,64,4096]{2,1,0:T(8,128)(2,1)S(1)}, u32[]{:S(2)}, u32[]{:S(2)}) %collective-permute-start.1) | collective-permute-done | bytes 1048608 | tf_op jit(solution)/shard_map/ppermute | solution.py:25
  (133 shorter events, 96.1 us)
Async XLA Ops:
  5.5 63.3 %copy-start.7 = (bf16[2,1,4,128,128]{4,3,2,1,0:T(8,128)(2,1)S(1)}, bf16[2,1,4,128,128]{4,3,2,1,0:T(8,128)(2,1)}, u32[]{:S(2)}) copy-start(bf16[2,1,4,128,128]{4,3,2,1,0:T(8,128)(2,1)} %param.14) | copy-start | bytes 786436
  5.5 63.3 %copy-start.9 = (s32[2,1,8,2]{2,3,1,0:T(2,128)S(1)}, s32[2,1,8,2]{2,3,1,0:T(2,128)}, u32[]{:S(2)}) copy-start(s32[2,1,8,2]{2,3,1,0:T(2,128)} %param.19) | copy-start | bytes 388
  5.5 61.1 %all-to-all-start = ((bf16[2,64,32,128]{3,1,0,2:T(8,128)(2,1)}), bf16[2,64,32,128]{3,1,0,2:T(8,128)(2,1)S(1)}, u32[]{:S(2)}, u32[]{:S(2)}) async-start(bf16[2,64,32,128]{3,1,0,2:T(8,128)(2,1)} %copy.69), calls=%async_computation | async-start | bytes 2097152 | tf_op jit(solution)/shard_map/all_to_all | solution.py:93
  78.9 1.6 copy-start
  106.7 1.6 copy-start
  124.5 19.7 %copy-start.8 = (bf16[2,1,16,32,32]{4,3,2,1,0:T(8,128)(2,1)S(1)}, bf16[2,1,16,32,32]{4,3,2,1,0:T(8,128)(2,1)}, u32[]{:S(2)}) copy-start(bf16[2,1,16,32,32]{4,3,2,1,0:T(8,128)(2,1)} %param.17) | copy-start | bytes 196612
  124.5 20.5 %copy-start.10 = (s32[2,1]{0,1:T(1,128)S(1)}, s32[2,1]{0,1:T(1,128)}, u32[]{:S(2)}) copy-start(s32[2,1]{0,1:T(1,128)} %param.18) | copy-start | bytes 28
  137.0 98.2 %all-to-all-start.1 = ((bf16[8,2,4,64,128]{4,3,2,1,0:T(8,128)(2,1)}), bf16[8,2,4,64,128]{4,3,2,1,0:T(8,128)(2,1)S(1)}, u32[]{:S(2)}, u32[]{:S(2)}) async-start(bf16[8,2,4,64,128]{4,3,2,1,0:T(8,128)(2,1)} %bitcast_dynamic-update-slice_fusion.8), calls=%async_computation.1 | async-start | bytes 2097152 | tf_op jit(solution)/shard_map/all_to_all | solution.py:13
  235.2 7.5 %copy-start.2 = (bf16[2,1,128,32,32]{3,4,2,0,1:T(8,128)(2,1)}, bf16[2,1,128,32,32]{3,4,2,0,1:T(8,128)(2,1)S(1)}, u32[]{:S(2)}) copy-start(bf16[2,1,128,32,32]{3,4,2,0,1:T(8,128)(2,1)S(1)} %all-gather) | copy-start | bytes 1572868
  248.0 1.9 copy-start.4
  251.2 52.9 %collective-permute-start = (bf16[2,64,4096]{2,1,0:T(8,128)(2,1)}, bf16[2,64,4096]{2,1,0:T(8,128)(2,1)S(1)}, u32[]{:S(2)}, u32[]{:S(2)}) collective-permute-start(bf16[2,64,4096]{2,1,0:T(8,128)(2,1)} %fusion.67), channel_id=1, source_target_pairs={{0,8},{8,16},{16,24},{24,32},{32,40},{40,48},{48,56},{56,64},{64,7... | collective-permute-start | bytes 3145736 | tf_op jit(solution)/shard_map/ppermute | solution.py:25
  304.7 1.0 copy-start.5
  307.0 57.8 %all-to-all-start.2 = ((bf16[2,64,32,128]{3,1,0,2:T(8,128)(2,1)}), bf16[2,64,32,128]{3,1,0,2:T(8,128)(2,1)S(1)}, u32[]{:S(2)}, u32[]{:S(2)}) async-start(bf16[2,64,32,128]{3,1,0,2:T(8,128)(2,1)} %copy_bitcast_fusion), calls=%async_computation.2 | async-start | bytes 2097152 | tf_op jit(solution)/shard_map/all_to_all | solution.py:93
  377.2 1.6 copy-start.1
  405.0 1.6 copy-start.1
  426.5 61.6 %copy-start.3 = (bf16[2,1,128,32,32]{3,4,2,0,1:T(8,128)(2,1)S(1)}, bf16[2,1,128,32,32]{3,4,2,0,1:T(8,128)(2,1)}, u32[]{:S(2)}) copy-start(bf16[2,1,128,32,32]{3,4,2,0,1:T(8,128)(2,1)} %copy-done.2) | copy-start | bytes 1572868
  496.8 1.6 copy-start.6
  500.3 62.3 %collective-permute-start.1 = (bf16[2,64,4096]{2,1,0:T(8,128)(2,1)S(1)}, bf16[2,64,4096]{2,1,0:T(8,128)(2,1)S(1)}, u32[]{:S(2)}, u32[]{:S(2)}) collective-permute-start(bf16[2,64,4096]{2,1,0:T(8,128)(2,1)S(1)} %fusion.66), channel_id=1, source_target_pairs={{0,8},{8,16},{16,24},{24,32},{32,40},{40,48},{48,56},{56,64},{64,7... | collective-permute-start | bytes 3145736 | tf_op jit(solution)/shard_map/ppermute | solution.py:25
